TPU v7x, 32 devices: a whole 2x2x4 slice. The times are simulated.
32 devices in a mesh: groups: 2 (over y), space: 4 (over x, core), chan: 4 (over z).
Axes of the slice: x: 2, y: 2, z: 4, core: 2. Of those that a mesh axis runs over, the one named last changes fastest.
Arguments:
- fields: bfloat16 [1024, 16, 256], P('chan', ('groups', 'space')), parts along dimension 1, may hold values from -6 to 6
- conv_weight: bfloat16 [27, 1024, 1024], P(None, 'chan', 'space'), may hold values from -0.0390625 to 0.0390625
Outputs:
- convolved: bfloat16 [1024, 16, 256], P('chan', ('groups', 'space')), parts along dimension 1
There are 2 independent parts, one for each index of `groups`. A program takes and returns all parts, laid end to end along the dimension named above; an argument that names none is the same for every part. Nothing has to cross between parts.
All inputs are finite; a program needn't handle non-finite values.
Results may differ from a plain program's by a relative error of at most 0.001.
Values may be sent and summed in bfloat16 or wider, within the bound.
A program may use at most 128 MiB of HBM per device.

v0:
```python
import functools

import jax
import jax.numpy as jnp
from jax import lax
from jax.experimental import pallas as pl
from jax.experimental.pallas import tpu as pltpu
from jax.sharding import PartitionSpec as P

NZ = 16
TAPS = 27
MESH = pl.DeviceIdType.MESH


def kernel(
    S, n, r, x_ref, w_ref, out_ref,
    xz, xr, xs, wv, psend, precv, xsend, xrecv, own,
    w_sem, up_sem, down_sem, z_sem, a_send, a_recv, p_send, p_recv, q_send, q_recv,
):
    depth, cells, chb = x_ref.shape
    I = r * chb
    nx = S // 2
    planes = S * depth
    s = lax.axis_index("space")
    z = lax.axis_index("chan")
    x = s // 2
    k = s % 2
    partner = x * 2 + (1 - k)

    for t in range(TAPS):
        pltpu.make_async_copy(w_ref.at[t], wv.at[:, t * I : (t + 1) * I], w_sem.at[t]).start()

    barrier = pltpu.get_barrier_semaphore()

    for so in range(S):
        for step, there in ((-1, z > 0), (1, z < n - 1)):
            @pl.when(there)
            def _():
                pl.semaphore_signal(
                    barrier, inc=1, device_id={"space": lax.rem(s + so, S), "chan": z + step},
                    device_id_type=MESH,
                )

    for so in range(1, S):
        pl.semaphore_signal(
            barrier, inc=1, device_id={"space": lax.rem(s + so, S)}, device_id_type=MESH
        )
    here = jnp.where(z > 0, S, 0) + jnp.where(z < n - 1, S, 0) + (S - 1)
    pl.semaphore_wait(barrier, here)

    split = cells // 2 + NZ
    spans = ((0, split), (split, cells - split))
    rows_out = cells // 2

    def part(ref, u):
        return ref.at[u % depth, pl.ds(*spans[u // depth])]

    def hop(src, b, p, sem, to):
        return pltpu.make_async_remote_copy(
            src_ref=src, dst_ref=part(xz.at[b], p), send_sem=sem, recv_sem=z_sem.at[b, p],
            device_id={"chan": to}, device_id_type=MESH,
        )

    def across(src, b, p):
        return pltpu.make_async_remote_copy(
            src_ref=src, dst_ref=part(xr.at[s, b % r], p), send_sem=a_send.at[b, p],
            recv_sem=a_recv.at[s, b % r, p],
            device_id={"space": b // r}, device_id_type=MESH,
        )

    def source(h, b, p):
        return part(x_ref, p) if h == 0 else part(xz.at[b], p)

    def up(h, p):
        return hop(source(h, z - h, p), z - h, p, up_sem.at[h, p], z + 1)

    def down(h, p):
        return hop(source(h, z + h, p), z + h, p, down_sem.at[h, p], z - 1)

    def slanted(h, b, p, sem, to):
        return pltpu.make_async_remote_copy(
            src_ref=source(h, b, p), dst_ref=part(xr.at[s, b % r], p), send_sem=sem,
            recv_sem=a_recv.at[s, b % r, p],
            device_id={"space": b // r, "chan": to}, device_id_type=MESH,
        )

    def direct(h, b, to, end):
        return (to == end) & (b // r != s)

    def forward(h, p):
        for b, sign, end, send in ((z - h, 1, n - 1, up), (z + h, -1, 0, down)):
            valid = (b >= 0) & (b < n)
            relay = valid
            if h > 0:
                relay = valid & (z != end)

                @pl.when(relay)
                def _():
                    hop(part(xz.at[b], p), b, p, up_sem.at[0, p], z).wait_recv()

            if h < n - 1:
                straight = direct(h, b, z + sign, end)

                @pl.when(valid & (z != end) & ~straight)
                def _():
                    send(h, p).start()

                @pl.when(valid & (z != end) & straight)
                def _():
                    sem = (up_sem if sign == 1 else down_sem).at[h, p]
                    slanted(h, b, p, sem, z + sign).start()

            if h > 0 or sign == 1:
                @pl.when(relay & (b // r != s))
                def _():
                    across(source(h, b, p), b, p).start()

    for p in range(2 * depth):
        forward(0, p)

    zero_row = jnp.zeros((NZ, I), xs.dtype)
    zero_plane = jnp.zeros(xs.shape[2:], xs.dtype)
    for c in range(3):
        xs[0, c] = zero_plane
        xs[planes + 1, c] = zero_plane

        @pl.loop(1, planes + 1)
        def _(q):
            xs[q, c, :NZ, :] = zero_row
            xs[q, c, NZ + cells :, :] = zero_row

    def prepare(ref, u, q, j):
        v = part(ref, u)[...]
        start, size = spans[u // depth]
        rows = lax.broadcasted_iota(jnp.int32, (size, chb), 0) % NZ
        wide = v.astype(jnp.float32)
        before = jnp.where(rows == 0, 0.0, pltpu.roll(wide, 1, 0))
        after = jnp.where(rows == NZ - 1, 0.0, pltpu.roll(wide, size - 1, 0))
        lanes = slice(j * chb, (j + 1) * chb)
        to = slice(NZ + start, NZ + start + size)
        xs[q + 1, 0, to, lanes] = before.astype(xs.dtype)
        xs[q + 1, 1, to, lanes] = v
        xs[q + 1, 2, to, lanes] = after.astype(xs.dtype)

    for half in range(2):
        for h in range(1, n - 1):
            for p in range(depth):
                forward(h, half * depth + p)

    def fetch_half(half):
        for p in range(depth):
            u = half * depth + p
            for j in range(r):
                @pl.when(z == s * r + j)
                def _():
                    prepare(x_ref, u, s * depth + p, j)

                b = s * r + j

                @pl.when(((z == 0) & (b > 0)) | ((z == n - 1) & (b < n - 1)))
                def _():
                    hop(part(xz.at[b], u), b, u, up_sem.at[0, u], z).wait_recv()

                @pl.when(z != s * r + j)
                def _():
                    prepare(xz.at[s * r + j], u, s * depth + p, j)

            @pl.loop(1, S)
            def _(so):
                src = lax.rem(s + so, S)
                for j in range(r):
                    view = part(xr.at[src, j], u)
                    pltpu.make_async_remote_copy(
                        src_ref=view, dst_ref=view,
                        send_sem=a_send.at[0, u], recv_sem=a_recv.at[src, j, u],
                        device_id={"space": src}, device_id_type=MESH,
                    ).wait_recv()
                    prepare(xr.at[src, j], u, src * depth + p, j)

    for t in range(TAPS):
        pltpu.make_async_copy(w_ref.at[t], wv.at[:, t * I : (t + 1) * I], w_sem.at[t]).wait()

    def partial(dest, half):
        window = jnp.concatenate(
            [
                jnp.concatenate(
                    [
                        xs[
                            dest * depth + p + a, c,
                            NZ * b + half * rows_out : NZ * b + (half + 1) * rows_out, :,
                        ]
                        for p in range(depth)
                    ],
                    axis=0,
                )
                for a in range(3)
                for b in range(3)
                for c in range(3)
            ],
            axis=1,
        )
        return lax.dot_general(
            window, wv[...], (((1,), (1,)), ((), ())), preferred_element_type=jnp.float32
        )

    def target(hops, mine):
        far = lax.rem(x + hops, nx)
        return far * 2 + jnp.where(mine == 1, k, 1 - k)

    def half_of(ref, m, half):
        return ref.at[m, half]

    def to_partner(m, half):
        return pltpu.make_async_remote_copy(
            src_ref=half_of(psend, m, half), dst_ref=half_of(precv, m, half),
            send_sem=p_send.at[m, half], recv_sem=p_recv.at[m, half],
            device_id={"space": partner}, device_id_type=MESH,
        )

    def to_chip(m, half, there):
        return pltpu.make_async_remote_copy(
            src_ref=half_of(xsend, m, half), dst_ref=half_of(xrecv, m, half),
            send_sem=q_send.at[m, half], recv_sem=q_recv.at[m, half],
            device_id={"space": there}, device_id_type=MESH,
        )

    def reduce_half(half, first, stop):
        @pl.loop(2 * first, 2 * stop)
        def _(i):
            m = i // 2
            mine = i % 2
            total = partial(target(m + 1, mine), half)

            @pl.when(mine == 0)
            def _():
                psend[m, half] = total
                to_partner(m, half).start()

            @pl.when(mine == 1)
            def _():
                to_partner(m, half).wait_recv()
                if first < nx - 1:
                    xsend[m, half] = total + precv[m, half]
                    to_chip(m, half, target(m + 1, 1)).start()
                else:
                    own[half] = total + precv[m, half]

    fetch_half(0)
    reduce_half(0, 0, nx - 1)
    fetch_half(1)
    reduce_half(1, 0, nx - 1)
    for half in range(2):
        reduce_half(half, nx - 1, nx)

    for half in range(2):
        total = own[half]
        for m in range(nx - 1):
            to_chip(m, half, partner).wait_recv()
            total = total + xrecv[m, half]
        for p in range(depth):
            out_ref[p, half * rows_out : (half + 1) * rows_out, :] = total[
                p * rows_out : (p + 1) * rows_out
            ].astype(out_ref.dtype)

    for h in range(n):
        for p in range(2 * depth):
            if h < n - 1:
                @pl.when((z - h >= 0) & (z < n - 1))
                def _():
                    up(h, p).wait_send()

                @pl.when((z + h < n) & (z > 0))
                def _():
                    down(h, p).wait_send()

            for b, sign, end in ((z - h, 1, n - 1), (z + h, -1, 0)):
                relay = (b >= 0) & (b < n) & (b // r != s)
                if h > 0:
                    relay = relay & ~direct(h - 1, b, z, end)

                if h > 0 or sign == 1:
                    @pl.when(relay)
                    def _():
                        across(source(h, b, p), b, p).wait_send()

    for m in range(nx):
        for half in range(2):
            to_partner(m, half).wait_send()
            if m < nx - 1:
                to_chip(m, half, partner).wait_send()


def local(S, n, fields, conv_weight):
    chb, depth, cells = fields.shape
    owned, I = conv_weight.shape[1:]
    r = I // chb
    nx = S // 2
    planes = S * depth
    bf16, f32 = jnp.bfloat16, jnp.float32
    dma = pltpu.SemaphoreType.DMA
    x = jnp.transpose(fields, (1, 2, 0))
    result = pl.pallas_call(
        functools.partial(kernel, S, n, r),
        out_shape=jax.ShapeDtypeStruct((depth, cells, owned), bf16),
        in_specs=[
            pl.BlockSpec(memory_space=pltpu.VMEM),
            pl.BlockSpec(memory_space=pl.ANY),
        ],
        out_specs=pl.BlockSpec(memory_space=pltpu.VMEM),
        scratch_shapes=[
            pltpu.VMEM((n, depth, cells, chb), bf16),
            pltpu.VMEM((S, r, depth, cells, chb), bf16),
            pltpu.VMEM((planes + 2, 3, cells + 2 * NZ, I), bf16),
            pltpu.VMEM((owned, TAPS * I), bf16),
            pltpu.VMEM((nx, 2, depth * cells // 2, owned), f32),
            pltpu.VMEM((nx, 2, depth * cells // 2, owned), f32),
            pltpu.VMEM((nx - 1, 2, depth * cells // 2, owned), f32),
            pltpu.VMEM((nx - 1, 2, depth * cells // 2, owned), f32),
            pltpu.VMEM((2, depth * cells // 2, owned), f32),
            dma((TAPS,)),
            dma((n, 2 * depth)),
            dma((n, 2 * depth)),
            dma((n, 2 * depth)),
            dma((n, 2 * depth)),
            dma((S, r, 2 * depth)),
            dma((nx, 2)),
            dma((nx, 2)),
            dma((nx, 2)),
            dma((nx, 2)),
        ],
        compiler_params=pltpu.CompilerParams(
            collective_id=0, has_side_effects=True, vmem_limit_bytes=62 * 1024 * 1024
        ),
    )(x, conv_weight)
    return jnp.transpose(result, (2, 0, 1))


def solution(mesh):
    return jax.shard_map(
        functools.partial(local, mesh.shape["space"], mesh.shape["chan"]),
        mesh=mesh,
        in_specs=(P("chan", ("groups", "space"), None), P(None, "chan", "space")),
        out_specs=P("chan", ("groups", "space"), None),
        check_vma=False,
    )
```

profile of v0, /device:TPU:0, one launch (start us, length us, event | category | flops | bytes accessed | tf_op | source)
XLA Modules:
  0.0 43.2 jit_solution(10540651312086534855)
XLA Ops:
  0.0 1.8 %copy.3 = bf16[256,2,256]{0,2,1:T(8,128)(2,1)} copy(bf16[256,2,256]{2,1,0:T(2,128)(2,1)} %param.2) | data formatting | bytes 524288 | tf_op args[0]
  1.8 39.5 %shard_map.28 = bf16[2,256,256]{2,1,0:T(8,128)(2,1)} custom-call(bf16[2,256,256]{2,1,0:T(8,128)(2,1)} %bitcast.3, bf16[27,256,256]{2,1,0:T(8,128)(2,1)} %w_ref.1), custom_call_target="tpu_custom_call" | custom-call | tf_op jit(solution)/shard_map/pallas_call | solution.py:302
  41.4 1.8 %copy.4 = bf16[256,2,256]{2,1,0:T(2,128)(2,1)} copy(bf16[256,2,256]{0,2,1:T(8,128)(2,1)} %bitcast.2) | data formatting | bytes 524288 | tf_op jit(solution)/shard_map/transpose | solution.py:335
where the time goes:
time: 43.4 us; the launch traced here: 43.2 us
  Pallas kernels  39.5 us (91%)
  local copies, waits for them, and re-layouts  3.63 us (8%)
    pallas_call x1, Pallas kernels, local(): pl.pallas_call(functools.partial(kernel, S, n, r), out_shape=jax.ShapeDty...  39.5 us
    transpose x1, local copies, waits for them, and re-layouts, local(): return jnp.transpose(result, (2, 0, 1))  1.82 us
    unnamed x1, local copies, waits for them, and re-layouts  1.81 us

commit v1 on v0

--- a/solution.py
+++ b/solution.py
@@ -12,7 +12,390 @@
 MESH = pl.DeviceIdType.MESH
 
 
+PIECES = 4
+
+
+def plan():
+    return [
+        ("F", 1, 0, 0), ("F", 1, 1, 0), ("P", 1, 0),
+        ("F", 3, 0, 0), ("F", 2, 0, 0), ("G", 0), ("XA", 0),
+        ("F", 3, 1, 0), ("F", 2, 1, 0), ("G", 1), ("XB", 0), ("XA", 1),
+        ("F", 1, 2, 0), ("F", 1, 3, 0), ("P", 1, 1),
+        ("F", 3, 2, 0), ("F", 2, 2, 0), ("G", 2), ("XB", 1), ("XA", 2),
+        ("F", 3, 3, 0), ("F", 2, 3, 0), ("G", 3), ("XB", 2), ("XA", 3),
+        ("F", 0, 0, 0), ("F", 0, 1, 0), ("XB", 3), ("P", 0, 0), ("YA", 0),
+        ("F", 0, 2, 0), ("F", 0, 3, 0), ("P", 0, 1), ("YA", 1), ("YB", 0), ("YB", 1),
+    ]
+
+
+def first():
+    return [
+        ("F", 1, 0), ("R", 0), ("F", 1, 1), ("F", 3, 0), ("F", 2, 0), ("R", 1), ("F", 3, 1), ("F", 2, 1),
+        ("F", 1, 2), ("R", 2), ("F", 3, 2), ("F", 2, 2), ("F", 1, 3), ("R", 3), ("F", 3, 3), ("F", 2, 3),
+        ("F", 0, 0), ("F", 0, 1), ("F", 0, 2), ("F", 0, 3),
+    ]
+
+
 def kernel(
+    S, n, x_ref, w_ref, out_ref,
+    xraw, xloc, xin, xrel, xs, wv, acc, precv, orecv, xsend, xrecv,
+    x_sem, w_sem, c_send, r_sem, u_send, d_send, l_send, l_recv, m_send,
+    p_send, p_recv, o_send, o_recv, q_send, q_recv,
+):
+    chb, depth, cells = x_ref.shape
+    planes = S * depth
+    half = cells // 2
+    piece = cells // PIECES
+    stops = [0] + [(q + 1) * piece + NZ for q in range(PIECES - 1)] + [cells]
+    spans = [(stops[q], stops[q + 1] - stops[q]) for q in range(PIECES)]
+    s = lax.axis_index("space")
+    z = lax.axis_index("chan")
+    x = s // 2
+    k = s % 2
+    partner = 2 * x + 1 - k
+    peer = 2 * (1 - x) + k
+    there = 2 * (1 - x) + 1 - k
+    source = s == z
+    goes_up = (z >= s) & (z < n - 1)
+    goes_down = (z <= s) & (z > 0)
+    edge = (s == 0) | (s == n - 1)
+    far_up = goes_up & (source | ~edge)
+    far_down = goes_down & (source | ~edge)
+    ahead = jnp.where(x == 1, 1, -1)
+    origin = jnp.where(x == 1, 0, n - 1)
+    feeds = z == origin
+    relays = z == origin + 2 * ahead
+    away = jnp.where(s == 0, z - s, s - z)
+
+    pltpu.make_async_copy(x_ref, xraw, x_sem).start()
+
+    barrier = pltpu.get_barrier_semaphore()
+
+    def greet(space, chan):
+        pl.semaphore_signal(
+            barrier, inc=1, device_id={"space": space, "chan": chan}, device_id_type=MESH
+        )
+
+    greet(partner, z)
+    greet(peer, z)
+
+    @pl.when(z > s)
+    def _():
+        greet(s, z - 1)
+
+    @pl.when(z < s)
+    def _():
+        greet(s, z + 1)
+
+    @pl.when(source)
+    def _():
+        for so in range(1, S):
+            greet(lax.rem(s + so, S), z)
+
+    @pl.when(relays)
+    def _():
+        greet(s, origin)
+
+    @pl.when(edge & (away >= 2))
+    def _():
+        row = jnp.where(s == 0, 2, n - 3)
+        for j in range(2):
+            greet(2 * (1 - x) + j, row)
+
+    for t in range(TAPS):
+        pltpu.make_async_copy(w_ref.at[t], wv.at[:, t * chb : (t + 1) * chb], w_sem.at[t]).start()
+
+    pltpu.make_async_copy(x_ref, xraw, x_sem).wait()
+    own = pltpu.einshape("cpm->pmc", xraw[...])
+    xloc[...] = own
+
+    @pl.when(source)
+    def _():
+        xin[s] = own
+
+    def one(flag):
+        return jnp.where(flag, 1, 0)
+
+    pl.semaphore_wait(
+        barrier,
+        2 + one(~source) + one(goes_up) + one(goes_down) + one(feeds) + 2 * one(relays),
+    )
+
+    def part(ref, p, q):
+        return ref.at[p, pl.ds(*spans[q])]
+
+    def gather(p, q):
+        return pltpu.make_async_remote_copy(
+            src_ref=part(xloc, p, q), dst_ref=part(xin.at[s], p, q), send_sem=c_send.at[p, q],
+            recv_sem=r_sem.at[s, p, q], device_id={"space": z}, device_id_type=MESH,
+        )
+
+    def feed(p, q):
+        return pltpu.make_async_remote_copy(
+            src_ref=part(xloc, p, q), dst_ref=part(xrel, p, q), send_sem=l_send.at[p, q],
+            recv_sem=l_recv.at[p, q], device_id={"chan": z + 2 * ahead}, device_id_type=MESH,
+        )
+
+    def relay(j, p, q):
+        return pltpu.make_async_remote_copy(
+            src_ref=part(xrel, p, q), dst_ref=part(xin.at[s], p, q), send_sem=m_send.at[j, p, q],
+            recv_sem=r_sem.at[s, p, q], device_id={"space": origin, "chan": z + j * ahead},
+            device_id_type=MESH,
+        )
+
+    def lane(b, p, q, sem, to):
+        view = part(xin.at[b], p, q)
+        return pltpu.make_async_remote_copy(
+            src_ref=view, dst_ref=view, send_sem=sem.at[b, p, q], recv_sem=r_sem.at[b, p, q],
+            device_id={"chan": to}, device_id_type=MESH,
+        )
+
+    def block(o):
+        return jnp.where(x == 0, o, S - 1 - o)
+
+    for q in range(PIECES):
+        for p in range(depth):
+            @pl.when(feeds)
+            def _():
+                feed(p, q).start()
+
+            @pl.when(~source)
+            def _():
+                gather(p, q).start()
+
+    def fetch(o, q):
+        b = block(o)
+        for p in range(depth):
+            @pl.when(b != jnp.where(source, s, S))
+            def _():
+                lane(b, p, q, u_send, lax.rem(z + 1, n)).wait_recv()
+
+            @pl.when(far_up if o >= 2 else goes_up)
+            def _():
+                lane(b, p, q, u_send, z + 1).start()
+
+            @pl.when(far_down if o >= 2 else goes_down)
+            def _():
+                lane(b, p, q, d_send, z - 1).start()
+
+    def pass_piece(q):
+        for p in range(depth):
+            feed(p, q).wait_recv()
+            for j in (1, 0):
+                relay(j, p, q).start()
+
+    def shifted(b, start, size):
+        rows = lax.broadcasted_iota(jnp.int32, (size, chb), 0) % NZ
+        to = slice(NZ + start, NZ + start + size)
+        for p in range(depth):
+            v = xin[b, p, start : start + size, :]
+            wide = v.astype(jnp.float32)
+            before = jnp.where(rows == 0, 0.0, pltpu.roll(wide, 1, 0))
+            after = jnp.where(rows == NZ - 1, 0.0, pltpu.roll(wide, size - 1, 0))
+            at = b * depth + p
+            xs[at, 0, to, :] = before.astype(xs.dtype)
+            xs[at, 1, to, :] = v
+            xs[at, 2, to, :] = after.astype(xs.dtype)
+
+    def multiply(base, count, start, size):
+        window = jnp.concatenate(
+            [
+                jnp.concatenate(
+                    [xs[base + p, c, NZ * y + start : NZ * y + start + size, :] for p in range(count)],
+                    axis=0,
+                )
+                for y in range(3)
+                for c in range(3)
+            ],
+            axis=1,
+        )
+        for a in range(3):
+            terms = lax.dot_general(
+                window, wv[:, a * 9 * chb : (a + 1) * 9 * chb], (((1,), (1,)), ((), ())),
+                preferred_element_type=jnp.float32,
+            )
+            acc[pl.ds(base + 2 - a, count), start : start + size, :] += terms.reshape(
+                count, size, chb
+            )
+
+    def near(o, h):
+        b = block(o)
+        start = 0 if h == 0 else stops[PIECES // 2]
+        stop = stops[PIECES // 2] if h == 0 else cells
+        shifted(b, start, stop - start)
+        multiply(b * depth, depth, h * half, half)
+
+    def distant(q):
+        for o in (3, 2):
+            shifted(block(o), *spans[q])
+        multiply(2 * (1 - x) * depth, 2 * depth, q * piece, piece)
+
+    def sums(core, start, size):
+        return acc.at[pl.ds(core * depth + 1, depth), start : start + size]
+
+    def far_piece(q):
+        return pltpu.make_async_remote_copy(
+            src_ref=sums(there, q * piece, piece), dst_ref=precv.at[q],
+            send_sem=p_send.at[q], recv_sem=p_recv.at[q],
+            device_id={"space": partner}, device_id_type=MESH,
+        )
+
+    def own_half(h):
+        return pltpu.make_async_remote_copy(
+            src_ref=sums(partner, h * half, half), dst_ref=orecv.at[h],
+            send_sem=o_send.at[h], recv_sem=o_recv.at[h],
+            device_id={"space": partner}, device_id_type=MESH,
+        )
+
+    def across(q):
+        return pltpu.make_async_remote_copy(
+            src_ref=xsend.at[q], dst_ref=xrecv.at[q], send_sem=q_send.at[q], recv_sem=q_recv.at[q],
+            device_id={"space": peer}, device_id_type=MESH,
+        )
+
+    def pass_on(q):
+        far_piece(q).wait_recv()
+        xsend[q] = sums(peer, q * piece, piece)[...] + precv[q]
+        across(q).start()
+
+    def finish(h):
+        own_half(h).wait_recv()
+        total = sums(s, h * half, half)[...] + orecv[h]
+        for j in range(PIECES // 2):
+            across(h * PIECES // 2 + j).wait_recv()
+        far = jnp.concatenate([xrecv[h * PIECES // 2 + j] for j in range(PIECES // 2)], axis=1)
+        total = total + far
+        wide = jnp.concatenate([total[p].T for p in range(depth)], axis=1)
+        out_ref[:, :, h * half : (h + 1) * half] = wide.reshape(chb, depth, half).astype(
+            out_ref.dtype
+        )
+
+    @pl.when(source)
+    def _():
+        for op in first():
+            if op[0] == "F":
+                fetch(*op[1:])
+            else:
+                @pl.when(relays)
+                def _():
+                    pass_piece(op[1])
+
+    zero_row = jnp.zeros((NZ, chb), xs.dtype)
+    for at in range(planes):
+        for c in range(3):
+            xs[at, c, :NZ, :] = zero_row
+            xs[at, c, NZ + cells :, :] = zero_row
+    for at in range(planes + 2):
+        acc[at] = jnp.zeros(acc.shape[1:], acc.dtype)
+
+    ready = False
+    for op in plan():
+        if op[0] == "F":
+            @pl.when(~source)
+            def _():
+                fetch(op[1], op[2])
+                if op[1] == 3:
+                    @pl.when(relays)
+                    def _():
+                        pass_piece(op[2])
+        if op[0] in ("P", "G") and not ready:
+            ready = True
+            for t in range(TAPS):
+                pltpu.make_async_copy(
+                    w_ref.at[t], wv.at[:, t * chb : (t + 1) * chb], w_sem.at[t]
+                ).wait()
+        if op[0] == "P":
+            near(*op[1:])
+        if op[0] == "G":
+            distant(op[1])
+        if op[0] == "XA":
+            far_piece(op[1]).start()
+        if op[0] == "XB":
+            pass_on(op[1])
+        if op[0] == "YA":
+            own_half(op[1]).start()
+        if op[0] == "YB":
+            finish(op[1])
+
+    for q in range(PIECES):
+        for p in range(depth):
+            @pl.when(feeds)
+            def _():
+                feed(p, q).wait_send()
+
+            @pl.when(~source)
+            def _():
+                gather(p, q).wait_send()
+
+            @pl.when(relays)
+            def _():
+                for j in range(2):
+                    relay(j, p, q).wait_send()
+
+            for o in range(S):
+                @pl.when(far_up if o >= 2 else goes_up)
+                def _():
+                    lane(block(o), p, q, u_send, lax.rem(z + 1, n)).wait_send()
+
+                @pl.when(far_down if o >= 2 else goes_down)
+                def _():
+                    lane(block(o), p, q, d_send, lax.rem(z + n - 1, n)).wait_send()
+
+        far_piece(q).wait_send()
+        across(q).wait_send()
+    for h in range(2):
+        own_half(h).wait_send()
+
+
+def local(S, n, fields, conv_weight):
+    chb, depth, cells = fields.shape
+    owned, I = conv_weight.shape[1:]
+    if not (S == n == 4 and owned == I == chb):
+        return general(S, n, fields, conv_weight)
+    planes = S * depth
+    bf16, f32 = jnp.bfloat16, jnp.float32
+    dma = pltpu.SemaphoreType.DMA
+    piece = cells // PIECES
+    return pl.pallas_call(
+        functools.partial(kernel, S, n),
+        out_shape=jax.ShapeDtypeStruct((owned, depth, cells), bf16),
+        in_specs=[pl.BlockSpec(memory_space=pl.ANY), pl.BlockSpec(memory_space=pl.ANY)],
+        out_specs=pl.BlockSpec(memory_space=pltpu.VMEM),
+        scratch_shapes=[
+            pltpu.VMEM((chb, depth, cells), bf16),
+            pltpu.VMEM((depth, cells, chb), bf16),
+            pltpu.VMEM((S, depth, cells, chb), bf16),
+            pltpu.VMEM((depth, cells, chb), bf16),
+            pltpu.VMEM((planes, 3, cells + 2 * NZ, chb), bf16),
+            pltpu.VMEM((owned, TAPS * chb), bf16),
+            pltpu.VMEM((planes + 2, cells, owned), f32),
+            pltpu.VMEM((PIECES, depth, piece, owned), f32),
+            pltpu.VMEM((2, depth, cells // 2, owned), f32),
+            pltpu.VMEM((PIECES, depth, piece, owned), f32),
+            pltpu.VMEM((PIECES, depth, piece, owned), f32),
+            dma(()),
+            dma((TAPS,)),
+            dma((depth, PIECES)),
+            dma((S, depth, PIECES)),
+            dma((S, depth, PIECES)),
+            dma((S, depth, PIECES)),
+            dma((depth, PIECES)),
+            dma((depth, PIECES)),
+            dma((2, depth, PIECES)),
+            dma((PIECES,)),
+            dma((PIECES,)),
+            dma((2,)),
+            dma((2,)),
+            dma((PIECES,)),
+            dma((PIECES,)),
+        ],
+        compiler_params=pltpu.CompilerParams(
+            collective_id=0, has_side_effects=True, vmem_limit_bytes=62 * 1024 * 1024
+        ),
+    )(fields, conv_weight)
+
+
+def general_kernel(
     S, n, r, x_ref, w_ref, out_ref,
     xz, xr, xs, wv, psend, precv, xsend, xrecv, own,
     w_sem, up_sem, down_sem, z_sem, a_send, a_recv, p_send, p_recv, q_send, q_recv,
@@ -290,7 +673,7 @@
                 to_chip(m, half, partner).wait_send()
 
 
-def local(S, n, fields, conv_weight):
+def general(S, n, fields, conv_weight):
     chb, depth, cells = fields.shape
     owned, I = conv_weight.shape[1:]
     r = I // chb
@@ -300,7 +683,7 @@
     dma = pltpu.SemaphoreType.DMA
     x = jnp.transpose(fields, (1, 2, 0))
     result = pl.pallas_call(
-        functools.partial(kernel, S, n, r),
+        functools.partial(general_kernel, S, n, r),
         out_shape=jax.ShapeDtypeStruct((depth, cells, owned), bf16),
         in_specs=[
             pl.BlockSpec(memory_space=pltpu.VMEM),

time: 43.4 us -> 42.6 us (0.982)
  local copies, waits for them, and re-layouts: 3.63 us -> 1.83 us
  Pallas kernels: 39.5 us -> 40.6 us
    transpose x1 -> x0, local copies, waits for them, and re-layouts: 1.82 us -> none  [local(): return jnp.transpose(result, (2, 0, 1))]
    pallas_call x1, Pallas kernels: 39.5 us -> 40.6 us  [local(): pl.pallas_call(functools.partial(kernel, S, n), out_shape=jax.ShapeDtypeS...]
where the time goes in v1:
time: 42.6 us; the launch traced here: 42.5 us
  Pallas kernels  40.6 us (95%)
  local copies, waits for them, and re-layouts  1.83 us (4%)
    pallas_call x1, Pallas kernels, local(): pl.pallas_call(functools.partial(kernel, S, n), out_shape=jax.ShapeDtypeS...  40.6 us
    unnamed x1, local copies, waits for them, and re-layouts  1.83 us

profile of v1, /device:TPU:0, one launch (start us, length us, event | category | flops | bytes accessed | tf_op | source)
XLA Modules:
  0.0 42.5 jit_solution(5954148130683764913)
XLA Ops:
  0.0 40.6 %shard_map.28 = bf16[256,2,256]{2,1,0:T(2,128)(2,1)} custom-call(bf16[256,2,256]{2,1,0:T(2,128)(2,1)} %x_ref.1, bf16[27,256,256]{2,1,0:T(8,128)(2,1)} %w_ref.1), custom_call_target="tpu_custom_call" | custom-call | tf_op jit(solution)/shard_map/pallas_call | solution.py:359
  40.6 1.8 %copy.4 = bf16[256,2,256]{2,1,0:T(2,128)(2,1)} copy(bf16[256,2,256]{2,1,0:T(2,128)(2,1)} %shard_map.28) | data formatting | bytes 524288

commit v2 on v1

--- a/solution.py
+++ b/solution.py
@@ -358,7 +358,7 @@
     piece = cells // PIECES
     return pl.pallas_call(
         functools.partial(kernel, S, n),
-        out_shape=jax.ShapeDtypeStruct((owned, depth, cells), bf16),
+        out_shape=pltpu.VMEM((owned, depth, cells), bf16),
         in_specs=[pl.BlockSpec(memory_space=pl.ANY), pl.BlockSpec(memory_space=pl.ANY)],
         out_specs=pl.BlockSpec(memory_space=pltpu.VMEM),
         scratch_shapes=[

time: 42.6 us -> 40.8 us (0.958)
  local copies, waits for them, and re-layouts: 1.83 us -> 0.71 us
  Pallas kernels: 40.6 us -> 39.9 us
    unnamed x1, local copies, waits for them, and re-layouts: 1.83 us -> 0.71 us
    pallas_call x1, Pallas kernels: 40.6 us -> 39.9 us  [local(): pl.pallas_call(functools.partial(kernel, S, n), out_shape=pltpu.VMEM((own...]
where the time goes in v2:
time: 40.8 us; the launch traced here: 40.7 us
  Pallas kernels  39.9 us (98%)
  local copies, waits for them, and re-layouts  0.71 us (2%)
    pallas_call x1, Pallas kernels, local(): pl.pallas_call(functools.partial(kernel, S, n), out_shape=pltpu.VMEM((own...  39.9 us

profile of v2, /device:TPU:0, one launch (start us, length us, event | category | flops | bytes accessed | tf_op | source)
XLA Modules:
  0.0 40.7 jit_solution(13796623614955254549)
XLA Ops:
  0.0 39.9 %shard_map.28 = bf16[256,2,256]{2,1,0:T(2,128)(2,1)S(1)} custom-call(bf16[256,2,256]{2,1,0:T(2,128)(2,1)} %x_ref.1, bf16[27,256,256]{2,1,0:T(8,128)(2,1)} %w_ref.1), custom_call_target="tpu_custom_call" | custom-call | tf_op jit(solution)/shard_map/pallas_call | solution.py:359
  40.0 0.7 %copy.4 = bf16[256,2,256]{2,1,0:T(2,128)(2,1)} copy(bf16[256,2,256]{2,1,0:T(2,128)(2,1)S(1)} %shard_map.28) | data formatting | bytes 524288

commit v3 on v2

--- a/solution.py
+++ b/solution.py
@@ -17,22 +17,67 @@
 
 def plan():
     return [
-        ("F", 1, 0, 0), ("F", 1, 1, 0), ("P", 1, 0),
-        ("F", 3, 0, 0), ("F", 2, 0, 0), ("G", 0), ("XA", 0),
-        ("F", 3, 1, 0), ("F", 2, 1, 0), ("G", 1), ("XB", 0), ("XA", 1),
-        ("F", 1, 2, 0), ("F", 1, 3, 0), ("P", 1, 1),
-        ("F", 3, 2, 0), ("F", 2, 2, 0), ("G", 2), ("XB", 1), ("XA", 2),
-        ("F", 3, 3, 0), ("F", 2, 3, 0), ("G", 3), ("XB", 2), ("XA", 3),
-        ("F", 0, 0, 0), ("F", 0, 1, 0), ("XB", 3), ("P", 0, 0), ("YA", 0),
-        ("F", 0, 2, 0), ("F", 0, 3, 0), ("P", 0, 1), ("YA", 1), ("YB", 0), ("YB", 1),
+        ('F', 1, 0, 0),
+        ('F', 1, 1, 0),
+        ('F', 1, 2, 0),
+        ('F', 1, 3, 0),
+        ('P', 1, 0),
+        ('F', 3, 0, 0),
+        ('F', 2, 0, 0),
+        ('P', 1, 1),
+        ('F', 3, 1, 0),
+        ('F', 2, 1, 0),
+        ('G', 0),
+        ('XA', 0),
+        ('F', 3, 2, 0),
+        ('F', 2, 2, 0),
+        ('G', 1),
+        ('XB', 0),
+        ('XA', 1),
+        ('F', 3, 3, 0),
+        ('F', 2, 3, 0),
+        ('G', 2),
+        ('XB', 1),
+        ('XA', 2),
+        ('F', 0, 0, 0),
+        ('F', 0, 1, 0),
+        ('G', 3),
+        ('XB', 2),
+        ('XA', 3),
+        ('F', 0, 2, 0),
+        ('F', 0, 3, 0),
+        ('P', 0, 0),
+        ('XB', 3),
+        ('YA', 0),
+        ('P', 0, 1),
+        ('YA', 1),
+        ('YB', 0),
+        ('YB', 1),
     ]
 
 
 def first():
     return [
-        ("F", 1, 0), ("R", 0), ("F", 1, 1), ("F", 3, 0), ("F", 2, 0), ("R", 1), ("F", 3, 1), ("F", 2, 1),
-        ("F", 1, 2), ("R", 2), ("F", 3, 2), ("F", 2, 2), ("F", 1, 3), ("R", 3), ("F", 3, 3), ("F", 2, 3),
-        ("F", 0, 0), ("F", 0, 1), ("F", 0, 2), ("F", 0, 3),
+        ('F', 1, 0),
+        ('F', 1, 1),
+        ('F', 1, 2),
+        ('F', 1, 3),
+        ('R', 0),
+        ('F', 3, 0),
+        ('F', 2, 0),
+        ('R', 1),
+        ('F', 3, 1),
+        ('F', 2, 1),
+        ('R', 2),
+        ('F', 3, 2),
+        ('F', 2, 2),
+        ('R', 3),
+        ('F', 3, 3),
+        ('F', 2, 3),
+        ('F', 0, 0),
+        ('F', 0, 1),
+        ('F', 0, 2),
+        ('F', 0, 3),
     ]
 
 
@@ -56,6 +101,8 @@
     peer = 2 * (1 - x) + k
     there = 2 * (1 - x) + 1 - k
     source = s == z
+    last = ~source & ((z == 0) | (z == n - 1))
+    middle = ~source & ~last
     goes_up = (z >= s) & (z < n - 1)
     goes_down = (z <= s) & (z > 0)
     edge = (s == 0) | (s == n - 1)
@@ -291,13 +338,25 @@
     ready = False
     for op in plan():
         if op[0] == "F":
-            @pl.when(~source)
+            @pl.when(middle)
             def _():
                 fetch(op[1], op[2])
                 if op[1] == 3:
                     @pl.when(relays)
                     def _():
                         pass_piece(op[2])
+        if op[0] in ("P", "G"):
+            needed = (
+                [(op[1], 2 * op[2]), (op[1], 2 * op[2] + 1)] if op[0] == "P"
+                else [(3, op[1]), (2, op[1])]
+            )
+
+            @pl.when(last)
+            def _():
+                for o, q in needed:
+                    for p in range(depth):
+                        lane(block(o), p, q, u_send, lax.rem(z + 1, n)).wait_recv()
+
         if op[0] in ("P", "G") and not ready:
             ready = True
             for t in range(TAPS):

time: 40.8 us -> 39 us (0.956)
  Pallas kernels: 39.9 us -> 38.2 us
    pallas_call x1, Pallas kernels: 39.9 us -> 38.2 us  [local(): pl.pallas_call(functools.partial(kernel, S, n), out_shape=pltpu.VMEM((own...]
where the time goes in v3:
time: 39 us; the launch traced here: 38.9 us
  Pallas kernels  38.2 us (98%)
  local copies, waits for them, and re-layouts  0.71 us (2%)
    pallas_call x1, Pallas kernels, local(): pl.pallas_call(functools.partial(kernel, S, n), out_shape=pltpu.VMEM((own...  38.2 us

profile of v3, /device:TPU:0, one launch (start us, length us, event | category | flops | bytes accessed | tf_op | source)
XLA Modules:
  0.0 38.9 jit_solution(18069034187648115604)
XLA Ops:
  0.0 38.2 %shard_map.28 = bf16[256,2,256]{2,1,0:T(2,128)(2,1)S(1)} custom-call(bf16[256,2,256]{2,1,0:T(2,128)(2,1)} %x_ref.1, bf16[27,256,256]{2,1,0:T(8,128)(2,1)} %w_ref.1), custom_call_target="tpu_custom_call" | custom-call | tf_op jit(solution)/shard_map/pallas_call | solution.py:418
  38.2 0.7 %copy.4 = bf16[256,2,256]{2,1,0:T(2,128)(2,1)} copy(bf16[256,2,256]{2,1,0:T(2,128)(2,1)S(1)} %shard_map.28) | data formatting | bytes 524288

commit v4 on v3

--- a/solution.py
+++ b/solution.py
@@ -45,11 +45,12 @@
         ('XB', 2),
         ('XA', 3),
         ('F', 0, 2, 0),
-        ('F', 0, 3, 0),
         ('P', 0, 0),
         ('XB', 3),
         ('YA', 0),
-        ('P', 0, 1),
+        ('F', 0, 3, 0),
+        ('Q', 0, 2),
+        ('Q', 0, 3),
         ('YA', 1),
         ('YB', 0),
         ('YB', 1),
@@ -202,13 +203,13 @@
 
     for q in range(PIECES):
         for p in range(depth):
+            @pl.when(~source)
+            def _():
+                gather(p, q).start()
+
             @pl.when(feeds)
             def _():
                 feed(p, q).start()
-
-            @pl.when(~source)
-            def _():
-                gather(p, q).start()
 
     def fetch(o, q):
         b = block(o)
@@ -345,8 +346,8 @@
                     @pl.when(relays)
                     def _():
                         pass_piece(op[2])
-        if op[0] in ("P", "G"):
-            needed = (
+        if op[0] in ("P", "G", "Q"):
+            needed = [op[1:3]] if op[0] == "Q" else (
                 [(op[1], 2 * op[2]), (op[1], 2 * op[2] + 1)] if op[0] == "P"
                 else [(3, op[1]), (2, op[1])]
             )
@@ -367,6 +368,10 @@
             near(*op[1:])
         if op[0] == "G":
             distant(op[1])
+        if op[0] == "Q":
+            b = block(op[1])
+            shifted(b, *spans[op[2]])
+            multiply(b * depth, depth, op[2] * piece, piece)
         if op[0] == "XA":
             far_piece(op[1]).start()
         if op[0] == "XB":

time: 39 us -> 38.8 us (level)
  no operation moved by 1% of the time
where the time goes in v4:
time: 38.8 us; the launch traced here: 38.7 us
  Pallas kernels  38 us (98%)
  local copies, waits for them, and re-layouts  0.71 us (2%)
    pallas_call x1, Pallas kernels, local(): pl.pallas_call(functools.partial(kernel, S, n), out_shape=pltpu.VMEM((own...  38 us

profile of v4, /device:TPU:0, one launch (start us, length us, event | category | flops | bytes accessed | tf_op | source)
XLA Modules:
  0.0 38.7 jit_solution(16562382124746639960)
XLA Ops:
  0.0 38.0 %shard_map.28 = bf16[256,2,256]{2,1,0:T(2,128)(2,1)S(1)} custom-call(bf16[256,2,256]{2,1,0:T(2,128)(2,1)} %x_ref.1, bf16[27,256,256]{2,1,0:T(8,128)(2,1)} %w_ref.1), custom_call_target="tpu_custom_call" | custom-call | tf_op jit(solution)/shard_map/pallas_call | solution.py:423
  38.0 0.7 %copy.4 = bf16[256,2,256]{2,1,0:T(2,128)(2,1)} copy(bf16[256,2,256]{2,1,0:T(2,128)(2,1)S(1)} %shard_map.28) | data formatting | bytes 524288
